TPU v7x, 32 devices: a whole 2x2x4 slice. The times are simulated.
32 devices in a mesh: dp: 4 (over y, x), seq: 8 (over z, core).
Axes of the slice: x: 2, y: 2, z: 4, core: 2. Of those that a mesh axis runs over, the one named last changes fastest.
Arguments:
- tokens: float32 [4, 1024, 1024], P('dp', 'seq'), may hold values from -6 to 6
- cotangent: float32 [4, 1024, 1024], P('dp', 'seq'), may hold values from -6 to 6
- doc_ids: int32 [4, 1024], P('dp'), may hold values from 0 to 1, never falling along the last dimension, each value on 1 to 768 neighbouring positions
- in_weight: float32 [1024, 4384], P(('dp', 'seq')), may hold values from -0.1875 to 0.1875
- out_weight: float32 [1024, 2048], P(('dp', 'seq')), may hold values from -0.125 to 0.125
- in_m: float32 [1024, 4384], P(('dp', 'seq')), may hold values from -30 to 30
- in_v: float32 [1024, 4384], P(('dp', 'seq')), may hold values from 1 to 1000
- out_m: float32 [1024, 2048], P(('dp', 'seq')), may hold values from -30 to 30
- out_v: float32 [1024, 2048], P(('dp', 'seq')), may hold values from 1 to 1000
- vec_params: float32 [14688], replicated, as said below
- vec_m: float32 [14688], replicated, may hold values from -30 to 30
- vec_v: float32 [14688], replicated, may hold values from 1 to 1000
Outputs:
- activations: float32 [4, 1024, 1024], P('dp', 'seq')
- input_grad: float32 [4, 1024, 1024], P('dp', 'seq')
- in_grad: float32 [1024, 4384], P(('dp', 'seq'))
- out_grad: float32 [1024, 2048], P(('dp', 'seq'))
- vec_grad: float32 [14688], replicated
- in_new: float32 [1024, 4384], P(('dp', 'seq'))
- out_new: float32 [1024, 2048], P(('dp', 'seq'))
- vec_new: float32 [14688], replicated
- in_m_new: float32 [1024, 4384], P(('dp', 'seq'))
- in_v_new: float32 [1024, 4384], P(('dp', 'seq'))
- out_m_new: float32 [1024, 2048], P(('dp', 'seq'))
- out_v_new: float32 [1024, 2048], P(('dp', 'seq'))
- vec_m_new: float32 [14688], replicated
- vec_v_new: float32 [14688], replicated
Inputs may be any that keep to these rules, and one draw needn't show every extreme that they name: `doc_ids`: each row holds document 0 and then document 1, each of one or more positions, none longer than 768. `vec_params`: norm_gain and gate_gain lie in 0.7 to 1.3, skip_gain in 0.5 to 1.5, step_bias in -1 to 1, log_rate in -12 to -3.
All inputs are finite; a program needn't handle non-finite values.
Results may differ from a plain program's by a relative error of at most 0.015.
Values may be sent and summed in bfloat16 or wider, within the bound.
A program may use at most 192 MiB of HBM per device.

v0:
```python
import jax
import jax.numpy as jnp
from jax import lax
from jax.experimental import pallas as pl
from jax.experimental.pallas import tpu as pltpu
from jax.sharding import PartitionSpec as P

D = 1024
DI = 2048
H = 32
P_SIZE = 64
N = 128
KW = 4
STRETCH = 256
STEP = 10
CONV = 2304


norm_eps = 1e-05
beta_one = 0.9
beta_two = 0.95
learn_rate = 0.03
decay_rate = 0.1
adam_eps = 1e-08
top_precision = lax.Precision.HIGHEST


def unpack(vector):
    cursor = D + DI
    norm_gain = vector[:D]
    gate_gain = vector[D:cursor]
    conv_kernel = vector[cursor : cursor + KW * CONV].reshape(KW, CONV)
    cursor = cursor + KW * CONV
    conv_bias = vector[cursor : cursor + CONV]
    cursor = cursor + CONV
    step_bias = vector[cursor : cursor + H]
    log_rate = vector[cursor + H : cursor + 2 * H]
    skip_gain = vector[cursor + 2 * H : cursor + 3 * H]
    return (norm_gain, gate_gain, conv_kernel, conv_bias, step_bias, log_rate, skip_gain)


def input_norm(inputs, gain):
    scale = lax.rsqrt(jnp.mean(inputs * inputs, axis=-1, keepdims=True) + norm_eps)
    return inputs * scale * gain[None, :]


def adamw_update(param, grad, first, second):
    first_new = beta_one * first + (1.0 - beta_one) * grad
    second_new = beta_two * second + (1.0 - beta_two) * grad * grad
    corrected = first_new / (1.0 - beta_one**STEP)
    scaled = jnp.sqrt(second_new / (1.0 - beta_two**STEP)) + adam_eps
    return (
        param * (1.0 - learn_rate * decay_rate) - learn_rate * corrected / scaled,
        first_new,
        second_new,
    )


CHUNK = 128
LANES = 128
bf16 = jnp.bfloat16
f32 = jnp.float32


def contract(a, b, left, right):
    return lax.dot_general(a, b, (((left,), (right,)), ((), ())), preferred_element_type=f32)


def spread_heads(table, heads, length):
    return jnp.concatenate(
        [jnp.broadcast_to(table[:, k : k + 1], (length, P_SIZE)) for k in range(heads)], axis=1
    )


def head_slice(block, k):
    return block[:, k * P_SIZE : (k + 1) * P_SIZE]


def chunk_terms(mixed_ref, raw_ref, meta_ref, ids_ref, small_ref, width):
    length = raw_ref.shape[0]
    values = mixed_ref[:, :width].astype(f32)
    input_map = mixed_ref[:, width : width + N]
    output_map = mixed_ref[:, width + N :]
    shifted_raw = raw_ref[...] + small_ref[0:1, :]
    step_size = jnp.maximum(shifted_raw, 0.0) + jnp.log1p(jnp.exp(-jnp.abs(shifted_raw)))
    rate = -jnp.exp(small_ref[1:2, :])
    log_decay = rate * step_size
    rows_index = lax.broadcasted_iota(jnp.int32, (length, length), 0)
    cols_index = lax.broadcasted_iota(jnp.int32, (length, length), 1)
    lower = rows_index >= cols_index
    cumulative = jnp.dot(
        lower.astype(f32), log_decay, precision=top_precision, preferred_element_type=f32
    )
    flipped = cumulative.T
    same = meta_ref[:, 0:1] == ids_ref[...]
    related = same & lower
    reach = meta_ref[:, 1:2] * jnp.exp(cumulative)
    tail = meta_ref[:, 2:3] * jnp.exp(cumulative[length - 1 :, :] - cumulative)
    scores = contract(output_map, input_map, 1, 1)

    def decay_of(k):
        spans = cumulative[:, k : k + 1] - flipped[k : k + 1, :]
        return jnp.exp(jnp.where(related, spans, -1e30))

    return (values, input_map, output_map, shifted_raw, step_size, rate, log_decay, same,
            rows_index, cols_index, reach, tail, scores, decay_of)


def position_table(ids, ext_ids):
    length = ids.shape[0]
    chunked = ids.reshape(-1, CHUNK)
    none = jnp.full((1,), -1, jnp.int32)
    prior = jnp.concatenate([none, chunked[:-1, -1]])[:, None]
    following = jnp.concatenate([chunked[1:, 0], none])[:, None]
    last = chunked[:, -1:]
    columns = [chunked, chunked == prior, chunked == last, chunked == following]
    columns = [column.astype(f32).reshape(-1) for column in columns]
    valid = [(ext_ids[offset : offset + length] == ids).astype(f32) for offset in range(KW - 1)]
    return jnp.pad(jnp.stack(columns + valid + [jnp.ones_like(columns[0])], axis=1), ((0, 8), (0, 0)))


MESH = pl.DeviceIdType.MESH
in_vmem = pl.BlockSpec(memory_space=pltpu.VMEM)


def beyond(axis, distance):
    count = lax.axis_size(axis)
    return lax.rem(lax.axis_index(axis) + distance + count, count)


def push(source, target, send_sem, recv_sem, axis, peer):
    return pltpu.make_async_remote_copy(
        src_ref=source, dst_ref=target, send_sem=send_sem, recv_sem=recv_sem,
        device_id={axis: peer}, device_id_type=MESH,
    )


def greet_all(axes):
    barrier = pltpu.get_barrier_semaphore()
    total = 0
    for axis in axes:
        for step in range(1, lax.axis_size(axis)):
            pl.semaphore_signal(barrier, inc=1, device_id={axis: beyond(axis, step)}, device_id_type=MESH)
            total += 1
    return lambda: pl.semaphore_wait(barrier, total)


def row_gather(seq_count, rows, right_send, right_recv, left_send, left_recv, core_send, core_recv):
    here = lax.axis_index("seq")
    chips = seq_count // 2
    chip, core = here // 2, lax.rem(here, 2)
    partner = here + 1 - 2 * core

    def right(k, peer):
        slot = here - 2 * (k - 1)
        return push(rows.at[slot], rows.at[slot], right_send.at[k], right_recv.at[k], "seq", peer)

    def left(k, peer):
        slot = here + 2 * (k - 1)
        return push(rows.at[slot], rows.at[slot], left_send.at[k], left_recv.at[k], "seq", peer)

    def across(q, slot):
        return push(rows.at[slot], rows.at[slot], core_send.at[q], core_recv.at[q], "seq", partner)

    def sends_right(k):
        return (chip < chips - 1) & (chip >= k - 1)

    def sends_left(k):
        return (chip > 0) & (chip + k <= chips)

    def send(k):
        if k < chips:
            @pl.when(sends_right(k))
            def _():
                right(k, here + 2).start()

            @pl.when(sends_left(k))
            def _():
                left(k, here - 2).start()

    def begin():
        send(1)
        across(chip, here).start()

    def stage(k):
        @pl.when(chip >= k)
        def _():
            slot = here - 2 * k
            push(rows.at[slot], rows.at[slot], right_send.at[k], right_recv.at[k], "seq", partner).wait_recv()

        @pl.when(chip + k < chips)
        def _():
            slot = here + 2 * k
            push(rows.at[slot], rows.at[slot], left_send.at[k], left_recv.at[k], "seq", partner).wait_recv()

        send(k + 1)

        @pl.when(chip >= k)
        def _():
            across(chip - k, here - 2 * k).start()

        @pl.when(chip + k < chips)
        def _():
            across(chip + k, here + 2 * k).start()

    def finish():
        for q in range(chips):
            across(q, 2 * q + 1 - core).wait_recv()
            across(q, 2 * q + core).wait_send()
        for k in range(1, chips):
            @pl.when(sends_right(k))
            def _(k=k):
                right(k, here + 2).wait_send()

            @pl.when(sends_left(k))
            def _(k=k):
                left(k, here - 2).wait_send()

    return begin, stage, finish


def row_scatter(seq_count, total, from_left, from_right, to_right, to_left, right_send, right_recv, left_send, left_recv):
    here = lax.axis_index("seq")
    chips = seq_count // 2
    chip = here // 2

    def right(source, q):
        return push(source.at[q], from_left.at[q], right_send.at[q], right_recv.at[q], "seq", here + 2)

    def left(source, q):
        return push(source.at[q], from_right.at[q], left_send.at[q], left_recv.at[q], "seq", here - 2)

    def begin():
        @pl.when(chip == 0)
        def _():
            for q in range(chips - 1, 0, -1):
                right(total, q).start()

        @pl.when(chip == chips - 1)
        def _():
            for q in range(chips - 1):
                left(total, q).start()

    def slot(t):
        for i in range(chips - 1):
            z = t - i
            q = chips - 1 - i
            if 1 <= z < q:
                @pl.when(chip == z)
                def _(q=q):
                    right(to_right, q).wait_recv()
                    to_right[q] = (total[q].astype(f32) + from_left[q].astype(f32)).astype(bf16)
                    right(to_right, q).start()

                @pl.when(chip == chips - 1 - z)
                def _(q=chips - 1 - q):
                    left(to_left, q).wait_recv()
                    to_left[q] = (total[q].astype(f32) + from_right[q].astype(f32)).astype(bf16)
                    left(to_left, q).start()

    def finish(acc):
        acc[...] = total[chip].astype(f32)

        @pl.when(chip > 0)
        def _():
            right(to_right, chip).wait_recv()
            acc[...] += from_left[chip].astype(f32)

        @pl.when(chip < chips - 1)
        def _():
            left(to_left, chip).wait_recv()
            acc[...] += from_right[chip].astype(f32)

        for q in range(chips):
            @pl.when(chip < q)
            def _(q=q):
                right(to_right, q).wait_send()

            @pl.when(chip > q)
            def _(q=q):
                left(to_left, q).wait_send()

    return begin, slot, finish


def scatter_scratch(block, chips):
    sems = pltpu.SemaphoreType.DMA
    return [pltpu.VMEM(block, bf16)] * 4 + [sems((chips,))] * 4


def spread_kernel(seq_count, dp_count, in_ref, last_ref, tok_ref, gain_ref, out, normed, blocks,
                  seq_send, seq_recv, dp_send, dp_recv, right_send, right_recv, left_send, left_recv,
                  core_send, core_recv):
    here, row = lax.axis_index("seq"), lax.axis_index("dp")
    arrive = greet_all(("seq", "dp"))
    width = DI // seq_count
    heads = H // seq_count
    mixed = width + 2 * N
    chips = seq_count // 2
    shared = in_ref[:, 2 * DI : DI + CONV].astype(bf16)
    step_cols = in_ref[:, DI + CONV :].astype(bf16)
    source = lax.broadcasted_iota(jnp.int32, (H, LANES), 0)
    target = lax.broadcasted_iota(jnp.int32, (H, LANES), 1)
    for p in range(seq_count):
        own = slice(p * width, (p + 1) * width)
        blocks[p, :, :width] = in_ref[:, own].astype(bf16)
        blocks[p, :, width : 2 * width] = in_ref[:, DI + p * width : DI + (p + 1) * width].astype(bf16)
        blocks[p, :, 2 * width : width + mixed] = shared
        chosen = ((source == target + p * heads) & (target < heads)).astype(bf16)
        blocks[p, :, width + mixed : width + mixed + LANES] = contract(step_cols, chosen, 1, 0).astype(bf16)
        blocks[p, :, width + mixed + LANES :] = last_ref[:, own].astype(bf16)
    arrive()

    def seq_copy(step, peer, slot):
        return push(blocks.at[peer], out.at[row, slot], seq_send.at[step], seq_recv.at[step], "seq", peer)

    def launch(step, _):
        seq_copy(step, beyond("seq", step), here).start()
        return 0

    lax.fori_loop(1, seq_count, launch, 0)
    out[row, here] = blocks[here]
    normed[here] = input_norm(tok_ref[...], gain_ref[...][0]).astype(bf16)

    begin, stage, finish_rows = row_gather(seq_count, normed, right_send, right_recv, left_send, left_recv, core_send, core_recv)
    quads = dp_count == 4

    def dp_copy(step, hop, from_row, source_ref):
        piece = beyond("seq", -step)
        return push(source_ref, out.at[from_row, piece], dp_send.at[step, hop], dp_recv.at[step, hop], "dp", flip(hop))

    def flip(hop):
        if not quads:
            return beyond("dp", hop)
        bit = hop if hop < 3 else 0
        low, high = lax.rem(row, 2), row // 2
        if bit == 1:
            return 2 * high + 1 - low
        return 2 * (1 - high) + low

    def origin(hop):
        if not quads:
            return beyond("dp", -hop)
        low, high = lax.rem(row, 2), row // 2
        return [row, 2 * high + 1 - low, 2 * (1 - high) + low, 3 - row][hop]

    def spread_own(step, from_blocks=False):
        piece = beyond("seq", -step)
        source_ref = blocks.at[here] if from_blocks else out.at[row, piece]
        for hop in (1, 2) if quads else range(1, dp_count):
            dp_copy(step, hop, row, source_ref).start()

    def relay_copy(step, via):
        piece = beyond("seq", -step)
        from_row = origin(via)
        return push(out.at[from_row, piece], out.at[from_row, piece], dp_send.at[step, 3], dp_recv.at[step, 3],
                    "dp", flip(3 - via))

    def relay(step):
        if not quads:
            return
        piece = beyond("seq", -step)

        for via in (1, 2):
            dp_copy(step, via, origin(via), out.at[row, piece]).wait_recv()

        @pl.when(lax.rem(step, 2) == 0)
        def _():
            relay_copy(step, 1).start()

        @pl.when(lax.rem(step, 2) == 1)
        def _():
            relay_copy(step, 2).start()

    spread_own(0, True)

    begin()

    def forward(step, _):
        seq_copy(step, beyond("seq", step), beyond("seq", -step)).wait_recv()
        spread_own(step)
        relay(step - 1)
        return 0

    lax.fori_loop(1, seq_count, forward, 0)

    for k in range(1, chips):
        stage(k)
        if k == 1:
            relay(seq_count - 1)
    if chips == 1:
        relay(seq_count - 1)

    def finish(step, _):
        piece = beyond("seq", -step)
        for hop in range(1, dp_count):
            if quads and hop < 3:
                dp_copy(step, hop, row, out.at[row, piece]).wait_send()
            else:
                copy = push(out.at[row, piece], out.at[origin(hop), piece], dp_send.at[step, hop],
                            dp_recv.at[step, hop], "dp", flip(hop))
                copy.wait_recv()
                copy.wait_send()

        @pl.when(step > 0)
        def _():
            seq_copy(step, beyond("seq", step), here).wait_send()

        return 0

    lax.fori_loop(0, seq_count, finish, 0)
    finish_rows()


def spread_weights(in_weight, out_weight, inputs, gain):
    seq_count, dp_count = lax.axis_size("seq"), lax.axis_size("dp")
    sems = pltpu.SemaphoreType.DMA
    width = DI // seq_count
    columns = 3 * width + 2 * N + LANES
    block = (seq_count, in_weight.shape[0], columns)
    chips = (seq_count // 2,)
    return pl.pallas_call(
        lambda *refs: spread_kernel(seq_count, dp_count, *refs),
        out_shape=[
            jax.ShapeDtypeStruct((dp_count,) + block, bf16),
            jax.ShapeDtypeStruct((seq_count,) + inputs.shape, bf16),
        ],
        in_specs=[in_vmem] * 4,
        out_specs=[in_vmem] * 2,
        scratch_shapes=[pltpu.VMEM(block, bf16)]
        + [sems((seq_count,))] * 2 + [sems((seq_count, dp_count))] * 2 + [sems(chips)] * 6,
        compiler_params=pltpu.CompilerParams(collective_id=1, has_side_effects=True),
        name="spread_weights",
    )(in_weight, out_weight, inputs, gain[None, :])


def rows_at(index, size):
    return pl.ds(pl.multiple_of(index * size, size), size)


def conv_window(conv_ref, c):
    return conv_ref[pl.ds(pl.multiple_of(c * CHUNK, CHUNK), CHUNK + 8), :]


def conv_before(window, table, kern_ref):
    taps = []
    total = kern_ref[KW : KW + 1, :]
    for k in range(KW):
        tap = window[8 - (KW - 1) + k : 8 - (KW - 1) + k + CHUNK, :]
        if k < KW - 1:
            tap = tap * table[:, 4 + k : 5 + k]
        taps.append(tap)
        total = total + kern_ref[k : k + 1, :] * tap
    return total, taps


def segments(count, parts):
    marks = [count * p // parts for p in range(parts + 1)]
    return list(zip(marks[:-1], marks[1:]))


def forward_kernel(seq_count, normed, weights, cotangent, table_ref, ids_ref, small_ref, kern_ref,
                   gate_ref, conv_ref, raw_ref, mixed_ref, ssd_ref, entry_ref, upstream,
                   state, *sems):
    heads = H // seq_count
    width = heads * P_SIZE
    mixed_width = width + 2 * N
    in_width = width + mixed_width + LANES
    length = normed.shape[0]
    here = lax.axis_index("seq")
    chips = seq_count // 2
    arrive = greet_all(("seq",))
    begin, stage, finish = row_gather(seq_count, upstream, *sems)
    upstream[here] = cotangent[...].astype(bf16)
    conv_ref[0:8, :] = jnp.zeros((8, mixed_width), f32)
    state[...] = jnp.zeros_like(state)
    arrive()
    begin()
    tall = 2 * CHUNK

    def project(i, _):
        out = contract(normed[rows_at(i, tall), :], weights[:, :in_width], 1, 0)
        gate_ref[rows_at(i, tall), :] = out[:, :width]
        conv_ref[pl.ds(pl.multiple_of(i * tall + 8, 8), tall), :] = out[:, width : width + mixed_width].astype(bf16).astype(f32)
        raw_ref[rows_at(i, tall), :] = out[:, width + mixed_width :]
        return 0

    lax.fori_loop(0, length // tall, project, 0)

    def chunk(c, _):
        table = table_ref[rows_at(c, CHUNK), :]
        before, _ = conv_before(conv_window(conv_ref, c), table, kern_ref)
        mixed = (before / (1.0 + jnp.exp(-before))).astype(bf16)
        mixed_ref[rows_at(c, CHUNK), :] = mixed
        (values, input_map, output_map, _, step_size, _, _, _, _, _, reach, tail, scores, decay_of) = (
            chunk_terms(mixed, raw_ref[rows_at(c, CHUNK), :], table, ids_ref[pl.ds(c, 1), :], small_ref, width)
        )
        entry = state[...]
        entry_low = entry.astype(bf16)
        entry_ref[c] = entry_low
        fed = (values * spread_heads(step_size, heads, CHUNK)).astype(bf16)
        inside = []
        for k in range(heads):
            mixing = (scores * decay_of(k)).astype(bf16)
            inside.append(contract(mixing, head_slice(fed, k), 1, 0))
        wide_reach = spread_heads(reach, heads, CHUNK)
        ssd_ref[rows_at(c, CHUNK), :] = jnp.concatenate(inside, axis=1) + wide_reach * contract(output_map, entry_low, 1, 0)
        weighted = (fed.astype(f32) * spread_heads(tail, heads, CHUNK)).astype(bf16)
        state[...] = entry * wide_reach[CHUNK - 1 :, :] + contract(input_map, weighted, 0, 0)
        return 0

    parts = segments(length // CHUNK, chips)
    for k, (low, high) in enumerate(parts):
        lax.fori_loop(low, high, chunk, 0)
        if k + 1 < chips:
            stage(k + 1)
    finish()


def shapes(*pairs):
    return [jax.ShapeDtypeStruct(shape, kind) for shape, kind in pairs]


def call(kernel, name, number, outs, scratch, operands, flops):
    params = dict(has_side_effects=True, collective_id=number, vmem_limit_bytes=60 * 1024 * 1024)
    return pl.pallas_call(
        kernel,
        out_shape=outs,
        in_specs=[in_vmem] * len(operands),
        out_specs=[in_vmem] * len(outs),
        scratch_shapes=scratch,
        compiler_params=pltpu.CompilerParams(**params),
        cost_estimate=pl.CostEstimate(flops=flops, bytes_accessed=8 * 1024 * 1024, transcendentals=0),
        name=name,
    )(*operands)


def forward(normed, weights, cotangent, table, ids, small, kern):
    seq_count = lax.axis_size("seq")
    length = normed.shape[0]
    width = DI // seq_count
    mixed_width = width + 2 * N
    count = length // CHUNK
    sems = pltpu.SemaphoreType.DMA
    outs = shapes(
        ((length, width), f32), ((length + 8, mixed_width), f32), ((length, LANES), f32), ((length, mixed_width), bf16),
        ((length, width), f32), ((count, N, width), bf16), ((seq_count,) + cotangent.shape, bf16),
    )
    scratch = [pltpu.VMEM((N, width), f32)] + [sems((seq_count // 2,))] * 6
    return call(lambda *refs: forward_kernel(seq_count, *refs), "forward", 2, outs, scratch,
                (normed, weights, cotangent, table, ids, small, kern), 2 * length * D * weights.shape[1])


def middle_kernel(seq_count, upstream, weights, ssd_ref, mixed_ref, gate_ref, gain_ref, skip_ref, normed,
                  total, grad_ref, low_ref, early, scale_ref, gain_grad, norm_row,
                  product_ref, gg_ref, part, arrived, theirs, got, out_low, send, recv, stat_send, stat_recv):
    width = DI // seq_count
    here = lax.axis_index("seq")
    chips = seq_count // 2
    core = lax.rem(here, 2)
    partner = here + 1 - 2 * core
    length = upstream.shape[0]
    count = length // CHUNK
    first = weights.shape[1] - width
    tall = 2 * CHUNK
    arrive = greet_all(("seq",))
    part[...] = jnp.zeros_like(part)
    line = lax.broadcasted_iota(jnp.int32, (2 * count, width), 0)

    def forward_part(i, _):
        at = rows_at(i, tall)
        gg = contract(upstream[at, :], weights[:, first:], 1, 0)
        gate_in = gate_ref[at, :]
        gate_act = gate_in / (1.0 + jnp.exp(-gate_in))
        product = (ssd_ref[at, :] + skip_ref[...] * mixed_ref[at, :width].astype(f32)) * gate_act
        product_ref[at, :] = product
        gg_ref[at, :] = gg
        square = product * product
        crossed = gg * gain_ref[...] * product
        sums = part[...]
        for half in range(2):
            rows = slice(half * CHUNK, (half + 1) * CHUNK)
            for offset, value in ((0, square), (count, crossed)):
                chosen = (line == 2 * i + half + offset).astype(f32)
                sums = sums + lax.dot_general(chosen, value[rows], (((1,), (1,)), ((), ())), precision=top_precision, preferred_element_type=f32)
        part[...] = sums
        return 0

    lax.fori_loop(0, length // tall, forward_part, 0)
    arrive()
    copies = [
        push(part, arrived.at[step], stat_send.at[step], stat_recv.at[step], "seq", beyond("seq", step))
        for step in range(1, seq_count)
    ]
    for copy in copies:
        copy.start()
    arrived[0] = part[...]
    long = total.shape[1]

    def term(piece):
        raw_out = (product_ref[rows_at(piece, long), :] * gain_ref[...]).astype(bf16)
        return contract(raw_out, weights[:, first:], 1, 1)

    def exchange(j):
        return push(theirs.at[j], got.at[j], send.at[j], recv.at[j], "seq", partner)

    def give(j, _):
        theirs[j] = term(2 * j + 1 - core).astype(bf16)

        @pl.when(j > 0)
        def _():
            exchange(j - 1).start()

        return 0

    lax.fori_loop(0, chips, give, 0)

    def keep(j, _):
        own = term(2 * j + core)

        @pl.when(j == 0)
        def _():
            exchange(chips - 1).start()

        exchange(j).wait_recv()
        total[j] = (own + got[j].astype(f32)).astype(bf16)
        return 0

    lax.fori_loop(0, chips, keep, 0)
    for copy in copies:
        copy.wait_recv()
    final = arrived[here]
    for origin in range(1, seq_count):
        final = final + arrived[lax.rem(here - origin + seq_count, seq_count)]
    scale = lax.rsqrt(final[:count] / DI + norm_eps)
    pull = scale * scale * scale * final[count:] / DI
    columns = jnp.concatenate([scale, pull], axis=0).T
    lane = lax.broadcasted_iota(jnp.int32, columns.shape, 1)
    scale_ref[...] = jnp.broadcast_to(
        jnp.sum(jnp.where(lane == here, columns, 0.0), axis=1, keepdims=True), scale_ref.shape
    )
    gain_grad[...] = jnp.zeros_like(gain_grad)

    def back(j, _):
        at = rows_at(j, CHUNK)
        own_scale = jnp.sum(jnp.where(lane == j, columns, 0.0), axis=1, keepdims=True)
        own_pull = jnp.sum(jnp.where(lane == j + count, columns, 0.0), axis=1, keepdims=True)
        gate_in = gate_ref[at, :]
        gate_sig = 1.0 / (1.0 + jnp.exp(-gate_in))
        ssd_out = ssd_ref[at, :] + skip_ref[...] * mixed_ref[at, :width].astype(f32)
        product = product_ref[at, :]
        gg = gg_ref[at, :]
        grad_product = gg * gain_ref[...] * own_scale - product * own_pull
        grad_ref[at, :] = grad_product * gate_in * gate_sig
        low_ref[at, :] = (grad_product * ssd_out * (gate_sig * (1.0 + gate_in * (1.0 - gate_sig)))).astype(bf16)
        gain_grad[0:1, :] += jnp.sum(gg * product * own_scale, axis=0, keepdims=True)
        raw_out = (product * gain_ref[...]).astype(bf16).astype(f32)
        out_low[at, :] = (raw_out * own_scale).astype(bf16)
        return 0

    lax.fori_loop(0, count, back, 0)

    def weigh(b, _):
        at = rows_at(b, tall)
        gate_grad = contract(normed[:, at], low_ref[...], 0, 0)
        early[at, :width] = gate_grad.astype(bf16)
        early[at, width:] = contract(upstream[:, at], out_low[...], 0, 0).astype(bf16)
        norm_row[:, at] = row_sums(weights[at, :width].astype(f32) * gate_grad)
        return 0

    lax.fori_loop(0, D // tall, weigh, 0)
    for j in range(chips):
        exchange(j).wait_send()
    for copy in copies:
        copy.wait_send()


def row_sums(matrix):
    ones = jnp.ones((8, matrix.shape[1]), f32)
    return lax.dot_general(ones, matrix, (((1,), (1,)), ((), ())), precision=top_precision, preferred_element_type=f32)


def middle(upstream, weights, ssd, mixed, gate_in, gain, skip, normed):
    seq_count = lax.axis_size("seq")
    length = upstream.shape[0]
    width = DI // seq_count
    chips = seq_count // 2
    count = length // CHUNK
    block = (chips, length // seq_count, D)
    sems = pltpu.SemaphoreType.DMA
    outs = shapes(
        (block, bf16), ((length, width), f32), ((length, width), bf16), ((D, 2 * width), bf16),
        ((length // seq_count, LANES), f32), ((8, width), f32), ((8, D), f32),
    )
    scratch = [
        pltpu.VMEM((length, width), f32), pltpu.VMEM((length, width), f32), pltpu.VMEM((2 * count, CHUNK), f32),
        pltpu.VMEM((seq_count, 2 * count, CHUNK), f32), pltpu.VMEM(block, bf16), pltpu.VMEM(block, bf16),
        pltpu.VMEM((length, width), bf16), sems((chips,)), sems((chips,)), sems((seq_count,)), sems((seq_count,)),
    ]
    return call(lambda *refs: middle_kernel(seq_count, *refs), "middle", 4, outs, scratch,
                (upstream, weights, ssd, mixed, gate_in, gain, skip, normed), 8 * length * D * width)


def backward_kernel(seq_count, dp_count, mixed_ref, raw_ref, table_ref, ids_ref, small_ref, skip_ref, ssd_ref, entry_ref,
                    grad_ref, conv_ref, kern_ref, out_total, early, scale_ref, tok_ref,
                    late_ref, totals_ref, gkern_ref, early_sum, out_ref,
                    later, carry, ahead, acc, early_got, early_send, early_recv, *chain):
    heads = H // seq_count
    width = heads * P_SIZE
    mixed_width = width + 2 * N
    length = raw_ref.shape[0]
    count = length // CHUNK
    chips = seq_count // 2
    row = lax.axis_index("dp")
    arrive = greet_all(("seq", "dp"))
    begin, slot, finish = row_scatter(seq_count, out_total, *chain)
    for ref in (later, carry, ahead, totals_ref, gkern_ref):
        ref[...] = jnp.zeros_like(ref)
    arrive()
    begin()

    def early_copy(hop):
        peer = beyond("dp", hop)
        return push(early.at[peer], early_got.at[hop], early_send.at[hop], early_recv.at[hop], "dp", peer)

    for hop in range(1, dp_count):
        early_copy(hop).start()
    channel = lax.broadcasted_iota(jnp.int32, (width, LANES), 0)
    lane = lax.broadcasted_iota(jnp.int32, (width, LANES), 1)
    member = ((channel >= lane * P_SIZE) & (channel < (lane + 1) * P_SIZE)).astype(f32)

    def per_head(wide):
        return jnp.dot(wide, member, precision=top_precision, preferred_element_type=f32)

    def chunk(turn, _):
        c = count - 1 - turn
        at = rows_at(c, CHUNK)
        table = table_ref[at, :]
        (values, input_map, output_map, shifted_raw, step_size, rate, log_decay, same, rows_index,
         cols_index, reach, tail, scores, decay_of) = chunk_terms(
            mixed_ref[at, :], raw_ref[at, :], table, ids_ref[pl.ds(c, 1), :], small_ref, width
        )
        grad = grad_ref[at, :]
        grad_low = grad.astype(bf16)
        wide_step = spread_heads(step_size, heads, CHUNK)
        wide_reach = spread_heads(reach, heads, CHUNK)
        wide_tail = spread_heads(tail, heads, CHUNK)
        fed = (values * wide_step).astype(bf16)
        fed_full = fed.astype(f32)
        after = later[...]
        after_low = after.astype(bf16)
        grad_scores = jnp.zeros((CHUNK, CHUNK), f32)
        pieces = []
        for k in range(heads):
            decay = decay_of(k)
            mixing = (scores * decay).astype(bf16)
            own_grad = head_slice(grad_low, k)
            grad_scores = grad_scores + contract(own_grad, head_slice(fed, k), 1, 1) * decay
            pieces.append(contract(mixing, own_grad, 0, 0))
        grad_fed = jnp.concatenate(pieces, axis=1) + wide_tail * contract(input_map, after_low, 1, 0)
        reached = (grad * wide_reach).astype(bf16)
        weighted = (fed_full * wide_tail).astype(bf16)
        scores_low = grad_scores.astype(bf16)
        grad_mixed = jnp.concatenate(
            [
                wide_step * grad_fed + skip_ref[...] * grad,
                contract(scores_low, output_map, 0, 0) + contract(weighted, after_low, 1, 1),
                contract(scores_low, input_map, 1, 0) + contract(reached, entry_ref[c], 1, 1),
            ],
            axis=1,
        )
        later[...] = after * wide_reach[CHUNK - 1 :, :] + contract(output_map, reached, 0, 0)
        balance = per_head(grad_low.astype(f32) * ssd_ref[at, :] - fed_full * grad_fed)
        grad_step = per_head(values * grad_fed)
        skip_total = per_head(jnp.broadcast_to(jnp.sum(values * grad, axis=0, keepdims=True), (8, width)))
        following = (same & (rows_index <= cols_index)).astype(f32)
        grad_log = jnp.dot(
            following, balance, precision=top_precision, preferred_element_type=f32
        ) + table[:, 3:4] * carry[0:1, :]
        carry[0:1, :] = grad_log[0:1, :]
        grad_step = grad_step + rate * grad_log
        grad_raw = grad_step * jax.nn.sigmoid(shifted_raw)
        totals_ref[0:1, :] += jnp.sum(grad_raw, axis=0, keepdims=True)
        totals_ref[1:2, :] += jnp.sum(grad_log * log_decay, axis=0, keepdims=True)
        totals_ref[2:3, :] += skip_total[0:1, :]
        before, taps = conv_before(conv_window(conv_ref, c), table, kern_ref)
        sig = 1.0 / (1.0 + jnp.exp(-before))
        grad_before = grad_mixed * (sig * (1.0 + before * (1.0 - sig)))
        for k in range(KW):
            gkern_ref[k : k + 1, :] += jnp.sum(grad_before * taps[k], axis=0, keepdims=True)
        gkern_ref[KW : KW + 1, :] += jnp.sum(grad_before, axis=0, keepdims=True)
        window = jnp.concatenate([grad_before, ahead[...]], axis=0)
        ahead[...] = grad_before[:8, :]
        wide_table = table_ref[pl.ds(pl.multiple_of(c * CHUNK, CHUNK), CHUNK + 8), :]
        grad_conv = kern_ref[KW - 1 : KW, :] * grad_before
        for k in range(KW - 1):
            shift = KW - 1 - k
            masked = window * wide_table[:, 4 + k : 5 + k]
            grad_conv = grad_conv + kern_ref[k : k + 1, :] * masked[shift : shift + CHUNK, :]
        late_ref[at, :mixed_width] = grad_conv.astype(bf16)
        late_ref[at, mixed_width:] = grad_raw.astype(bf16)
        return 0

    parts = segments(count, chips - 1) if chips > 1 else [(0, count)]
    for t, (low, high) in enumerate(parts):
        lax.fori_loop(low, high, chunk, 0)
        if t + 1 < chips - 1:
            slot(t + 1)
    for hop in range(1, dp_count):
        early_copy(hop).wait_recv()

    def combine(piece, _):
        value = early[row, piece].astype(f32)
        for hop in range(1, dp_count):
            value = value + early_got[hop, piece].astype(f32)
        early_sum[piece] = value.astype(bf16)
        return 0

    lax.fori_loop(0, seq_count, combine, 0)
    finish(acc)
    out_ref[...] = tok_ref[...] + acc[...] * scale_ref[:, 0:1]
    for hop in range(1, dp_count):
        early_copy(hop).wait_send()


def backward(mixed, raw, table, ids, small, skip, ssd, entries, grad, conv_in, kern, out_total, early, scale, tokens):
    seq_count, dp_count = lax.axis_size("seq"), lax.axis_size("dp")
    length = raw.shape[0]
    width = DI // seq_count
    mixed_width = width + 2 * N
    sems = pltpu.SemaphoreType.DMA
    outs = shapes(
        ((length, mixed_width + LANES), bf16), ((8, LANES), f32), ((8, mixed_width), f32),
        (early.shape[1:], bf16), (tokens.shape, f32),
    )
    scratch = [
        pltpu.VMEM((N, width), f32), pltpu.VMEM((8, LANES), f32), pltpu.VMEM((8, mixed_width), f32), pltpu.VMEM(tokens.shape, f32),
        pltpu.VMEM(early.shape, bf16), sems((dp_count,)), sems((dp_count,)),
    ] + scatter_scratch(out_total.shape, seq_count // 2)
    return call(lambda *refs: backward_kernel(seq_count, dp_count, *refs), "backward", 5, outs, scratch,
                (mixed, raw, table, ids, small, skip, ssd, entries, grad, conv_in, kern, out_total, early, scale, tokens),
                16 * length * N * width)


def final_kernel(seq_count, dp_count, lines, low_ref, late_ref, weights, normed, early, gain_ref, norm_row, gain_grad,
                 gkern_ref, totals_ref, tok_ref, cot_ref,
                 returned, returned_early, vec_out, in_grad_ref,
                 total, theirs, got_rows, part, got, summed, vec, vec_dp, vec_row, vec_seq, acc,
                 pair_send, pair_recv, dp_send, dp_recv, seq_send, seq_recv, early_send, early_recv,
                 va_send, va_recv, vb_send, vb_recv, vc_send, vc_recv, vd_send, vd_recv, *chain):
    here, row = lax.axis_index("seq"), lax.axis_index("dp")
    heads = H // seq_count
    width = DI // seq_count
    mixed_width = width + 2 * N
    in_width = width + mixed_width + LANES
    chips = seq_count // 2
    core = lax.rem(here, 2)
    partner = here + 1 - 2 * core
    hops = range(1, dp_count)
    steps = range(1, seq_count)
    tall = 2 * CHUNK
    share = part.shape[1]
    begin, slot, finish_rows = row_scatter(seq_count, total, *chain)
    arrive = greet_all(("seq", "dp"))
    arrive()

    def early_copy(step, place):
        piece = beyond("seq", step)
        return push(early.at[piece], returned_early.at[place], early_send.at[step], early_recv.at[step], "seq", piece)

    for step in steps:
        early_copy(step, here).start()
    returned_early[here] = early[here]

    long = total.shape[1]

    def term(piece):
        at = rows_at(piece, long)
        return contract(low_ref[at, :], weights[:, :width], 1, 1) + contract(late_ref[at, :], weights[:, width:in_width], 1, 1)

    def pair(j):
        return push(theirs.at[j], got_rows.at[j], pair_send.at[j], pair_recv.at[j], "seq", partner)

    def give(j, _):
        theirs[j] = term(2 * j + 1 - core).astype(bf16)

        @pl.when(j > 0)
        def _():
            pair(j - 1).start()

        return 0

    lax.fori_loop(0, chips, give, 0)

    def keep(j, _):
        own = term(2 * j + core)

        @pl.when(j == 0)
        def _():
            pair(chips - 1).start()

        pair(j).wait_recv()
        total[j] = (own + got_rows[j].astype(f32)).astype(bf16)
        return 0

    lax.fori_loop(0, chips, keep, 0)
    begin()

    vec[...] = jnp.zeros_like(vec)

    def weigh(b, _):
        at = rows_at(b, tall)
        grads = contract(normed[:, at], late_ref[...], 0, 0)
        for i in range(tall // share):
            part[b * (tall // share) + i] = grads[i * share : (i + 1) * share, :].astype(bf16)
        sums = row_sums(weights[at, width:in_width].astype(f32) * grads)
        sums = (sums + norm_row[:, at]) / gain_ref[:, at]
        for j in range(tall // LANES):
            vec[pl.ds(b * (tall // LANES) + j, 1), :] = sums[0:1, j * LANES : (j + 1) * LANES]
        return 0

    lax.fori_loop(0, D // tall, weigh, 0)

    def write(base, source, line, columns, moving):
        for j in range(columns[0] // LANES, columns[1] // LANES):
            at = base + j - columns[0] // LANES
            if moving:
                at = at + here * (width // LANES)
            vec[pl.ds(at, 1), :] = source[line : line + 1, j * LANES : (j + 1) * LANES]

    base = D // LANES
    write(base, gain_grad, 0, (0, width), True)
    base += DI // LANES
    for k in range(KW + 1):
        write(base, gkern_ref, k, (0, width), True)
        write(base + DI // LANES, gkern_ref, k, (width, mixed_width), False)
        base += CONV // LANES
    source = lax.broadcasted_iota(jnp.int32, (LANES, LANES), 0)
    target = lax.broadcasted_iota(jnp.int32, (LANES, LANES), 1)
    tail = jnp.zeros((8, LANES), f32)
    picked = lax.broadcasted_iota(jnp.int32, (8, LANES), 0)
    sums = totals_ref[...]
    for k in range(3):
        chosen = ((target == source + k * H + here * heads) & (source < heads)).astype(f32)
        tail = tail + jnp.dot(jnp.where(picked == k, sums, 0.0), chosen, precision=top_precision, preferred_element_type=f32)
    vec[base : base + 1, :] = jnp.sum(tail, axis=0, keepdims=True)

    wide = seq_count * lines
    first = [push(vec.at[rows_at(beyond("dp", hop), wide), :], vec_dp.at[hop], va_send.at[hop], va_recv.at[hop], "dp", beyond("dp", hop)) for hop in hops]
    for copy in first:
        copy.start()
    def dp_copy(step, hop):
        piece = beyond("seq", step)
        peer = beyond("dp", hop)
        return push(part.at[peer * seq_count + piece], got.at[hop, piece], dp_send.at[step, hop], dp_recv.at[step, hop], "dp", peer)

    def launch(step, _):
        for hop in hops:
            dp_copy(lax.rem(step, seq_count), hop).start()
        return 0

    lax.fori_loop(1, seq_count + 1, launch, 0)
    for copy in first:
        copy.wait_recv()
    value = vec[rows_at(row, wide), :]
    for hop in hops:
        value = value + vec_dp[hop]
    vec_row[...] = value
    second = [push(vec_row.at[rows_at(beyond("seq", step), lines), :], vec_seq.at[step], vb_send.at[step], vb_recv.at[step], "seq", beyond("seq", step)) for step in steps]
    for copy in second:
        copy.start()
    if chips > 2:
        slot(1)

    def seq_copy(step, place):
        piece = beyond("seq", step)
        return push(summed.at[piece], returned.at[place], seq_send.at[step], seq_recv.at[step], "seq", piece)

    def combined(step):
        piece = beyond("seq", step)
        for hop in hops:
            dp_copy(step, hop).wait_recv()
        value = part[row * seq_count + piece].astype(f32)
        for hop in hops:
            value = value + got[hop, piece].astype(f32)
        return value.astype(bf16)

    def swap(step, _):
        summed[beyond("seq", step)] = combined(step)
        seq_copy(step, here).start()
        return 0

    half = seq_count // 2
    lax.fori_loop(1, half, swap, 0)
    for copy in second:
        copy.wait_recv()
    final = vec_row[rows_at(here, lines), :]
    for step in steps:
        final = final + vec_seq[step]
    spot = row * seq_count + here
    vec_out[rows_at(spot, lines), :] = final

    def third(step, place):
        at = rows_at(row * seq_count + place, lines)
        return push(vec_out.at[rows_at(spot, lines), :], vec_out.at[at, :], vc_send.at[step], vc_recv.at[step], "seq", beyond("seq", step))

    for step in steps:
        third(step, here).start()
    for t in range(2, chips - 1):
        slot(t)
    lax.fori_loop(half, seq_count, swap, 0)
    returned[here] = combined(0)
    for step in steps:
        third(step, beyond("seq", -step)).wait_recv()

    def fourth(hop, place):
        return push(vec_out.at[rows_at(row, wide), :], vec_out.at[rows_at(place, wide), :], vd_send.at[hop], vd_recv.at[hop], "dp", beyond("dp", hop))

    for hop in hops:
        fourth(hop, row).start()
    finish_rows(acc)
    inputs = tok_ref[...]
    scale = lax.rsqrt(jnp.mean(inputs * inputs, axis=-1, keepdims=True) + norm_eps)
    pulled = acc[...] * gain_ref[...]
    dots = jnp.sum(pulled * inputs, axis=-1, keepdims=True)
    in_grad_ref[...] = cot_ref[...] + scale * pulled - inputs * (scale * scale * scale * dots / D)

    def close(step, _):
        seq_copy(step, beyond("seq", -step)).wait_recv()
        seq_copy(step, here).wait_send()
        early_copy(step, beyond("seq", -step)).wait_recv()
        early_copy(step, here).wait_send()
        return 0

    lax.fori_loop(1, seq_count, close, 0)

    def drain(step, _):
        for hop in hops:
            dp_copy(step, hop).wait_send()
        return 0

    lax.fori_loop(0, seq_count, drain, 0)
    for hop in hops:
        fourth(hop, beyond("dp", -hop)).wait_recv()
        fourth(hop, row).wait_send()
    for copy in first + second:
        copy.wait_send()
    for step in steps:
        third(step, here).wait_send()
    for j in range(chips):
        pair(j).wait_send()


def final(low, late, weights, normed, early, gain, norm_row, gain_grad, gkern, totals, tokens, cotangent):
    seq_count, dp_count = lax.axis_size("seq"), lax.axis_size("dp")
    devices = seq_count * dp_count
    chips = seq_count // 2
    vec_size = D + DI + (KW + 1) * CONV + 3 * H
    lines = -(-vec_size // (devices * LANES * 8)) * 8
    share = D // devices
    columns = late.shape[1]
    block = (chips,) + tokens.shape
    sems = pltpu.SemaphoreType.DMA
    outs = shapes(
        ((seq_count, share, columns), bf16), (early.shape, bf16), ((devices * lines, LANES), f32), (tokens.shape, f32)
    )
    scratch = [
        pltpu.VMEM(block, bf16), pltpu.VMEM(block, bf16), pltpu.VMEM(block, bf16), pltpu.VMEM((devices, share, columns), bf16),
        pltpu.VMEM((dp_count, seq_count, share, columns), bf16), pltpu.VMEM((seq_count, share, columns), bf16),
        pltpu.VMEM((devices * lines, LANES), f32), pltpu.VMEM((dp_count, seq_count * lines, LANES), f32),
        pltpu.VMEM((seq_count * lines, LANES), f32), pltpu.VMEM((seq_count, lines, LANES), f32), pltpu.VMEM(tokens.shape, f32),
    ]
    counts = [(chips,)] * 2 + [(seq_count, dp_count)] * 2 + [(seq_count,)] * 4 + [(dp_count,)] * 2 + [(seq_count,)] * 4 + [(dp_count,)] * 2
    scratch += [sems(shape) for shape in counts] + scatter_scratch(block, chips)
    return call(lambda *refs: final_kernel(seq_count, dp_count, lines, *refs), "final", 3, outs, scratch,
                (low, late, weights, normed, early, gain, norm_row, gain_grad, gkern, totals, tokens, cotangent),
                4 * D * D * columns)


def body(tokens, cotangent, doc_ids, in_weight, out_weight, in_m, in_v, out_m, out_v, vec_params, vec_m, vec_v):
    seq_count = lax.axis_size("seq")
    place = lax.axis_index("seq")
    heads = H // seq_count
    width = DI // seq_count
    mixed_width = width + 2 * N
    owner_rows = in_weight.shape[0]
    inputs = tokens[0]
    upstream_f = cotangent[0]
    norm_gain = vec_params[:D]

    weights, normed_all = spread_weights(in_weight, out_weight, inputs, norm_gain)
    weights = weights.reshape(D, -1)
    normed_all = normed_all.reshape(-1, D)
    _, gate_gain, conv_kernel, conv_bias, step_bias, log_rate, skip_gain = unpack(vec_params)
    ids = doc_ids[0]
    ext_ids = jnp.concatenate([jnp.full((KW - 1,), -1, jnp.int32), ids])
    table = position_table(ids, ext_ids)
    ids_rows = ids.astype(f32).reshape(-1, CHUNK)

    def own(vector, size):
        return lax.dynamic_slice_in_dim(vector, place * size, size, vector.ndim - 1)

    own_gain = own(gate_gain, width)[None, :]
    both = jnp.concatenate([conv_kernel, conv_bias[None, :]])
    kern = jnp.pad(jnp.concatenate([own(both[:, :DI], width), both[:, DI:]], axis=1), ((0, 7 - KW), (0, 0)))
    wide_skip = jnp.repeat(own(skip_gain, heads), P_SIZE)[None, :]
    small = jnp.pad(jnp.stack([own(step_bias, heads), own(log_rate, heads)]), ((0, 6), (0, LANES - heads)))

    gate_in, conv_in, raw, mixed, ssd, entries, upstream_all = forward(
        normed_all, weights, upstream_f, table, ids_rows, small, kern
    )
    upstream_all = upstream_all.reshape(-1, D)
    out_total, grad_ssd, gate_low, early, scale, gain_grad, norm_row = middle(
        upstream_all, weights, ssd, mixed, gate_in, own_gain, wide_skip, normed_all
    )
    early = early.reshape(lax.axis_size("dp"), seq_count, owner_rows, -1)
    late, totals, gkern, early, outputs = backward(
        mixed, raw, table, ids_rows, small, wide_skip, ssd, entries, grad_ssd, conv_in, kern, out_total, early, scale, inputs
    )
    returned, returned_early, vec_sum, input_grad = final(
        gate_low, late, weights, normed_all, early, norm_gain[None, :], norm_row, gain_grad, gkern, totals, inputs, upstream_f
    )
    returned = returned.astype(f32)
    returned_early = returned_early.astype(f32)
    vec_grad = vec_sum.reshape(-1)[: vec_params.shape[0]]

    def gathered(array, start, size):
        return array[:, :, start : start + size].transpose(1, 0, 2).reshape(owner_rows, -1)

    in_grad = jnp.concatenate(
        [
            gathered(returned_early, 0, width),
            gathered(returned, 0, width),
            jnp.sum(returned[:, :, width : width + 2 * N], axis=0),
            gathered(returned, mixed_width, heads),
        ],
        axis=1,
    )
    out_grad = gathered(returned_early, width, width)

    in_new, in_m_new, in_v_new = adamw_update(in_weight, in_grad, in_m, in_v)
    out_new, out_m_new, out_v_new = adamw_update(out_weight, out_grad, out_m, out_v)
    vec_new, vec_m_new, vec_v_new = adamw_update(vec_params, vec_grad, vec_m, vec_v)
    return (
        outputs[None],
        input_grad[None],
        in_grad,
        out_grad,
        vec_grad,
        in_new,
        out_new,
        vec_new,
        in_m_new,
        in_v_new,
        out_m_new,
        out_v_new,
        vec_m_new,
        vec_v_new,
    )


def solution(mesh):
    in_specs = (
        P("dp", "seq", None),
        P("dp", "seq", None),
        P("dp", None),
        P(("dp", "seq"), None),
        P(("dp", "seq"), None),
        P(("dp", "seq"), None),
        P(("dp", "seq"), None),
        P(("dp", "seq"), None),
        P(("dp", "seq"), None),
        P(),
        P(),
        P(),
    )
    out_specs = (
        P("dp", "seq", None),
        P("dp", "seq", None),
        P(("dp", "seq"), None),
        P(("dp", "seq"), None),
        P(),
        P(("dp", "seq"), None),
        P(("dp", "seq"), None),
        P(),
        P(("dp", "seq"), None),
        P(("dp", "seq"), None),
        P(("dp", "seq"), None),
        P(("dp", "seq"), None),
        P(),
        P(),
    )
    return jax.shard_map(body, mesh=mesh, in_specs=in_specs, out_specs=out_specs, check_vma=False)
```

profile of v0, /device:TPU:1, one launch (start us, length us, event | category | flops | bytes accessed | tf_op | source)
XLA Modules:
  0.0 191.0 jit_solution(2553770125307214430)
XLA Ops:
  0.6 0.9 slice_reduce_fusion.2
  1.5 1.0 slice_reduce_fusion.1
  2.5 0.1 pad_add_fusion
  2.6 0.9 fusion.13
  3.5 0.1 dynamic_slice.18
  3.5 0.1 dynamic-slice_bitcast_fusion
  3.6 0.1 broadcast_in_dim.23
  3.7 0.6 broadcast_in_dim_reshape.3.refs_6_.refs_5_
  4.3 0.6 select_maximum_fusion.1.refs_5_.refs_4_
  4.9 0.1 eq.62
  5.0 0.1 eq.66
  5.1 1.3 convert_element_type.63.refs_4_.refs_3_
  6.3 0.1 eq.69
  6.4 0.7 compare_convert_fusion
  7.1 0.7 bitcast_convert_fusion
  7.8 1.3 slice.63
  9.1 0.7 slice.77
  9.8 0.6 dynamic_slice.19
  10.4 0.7 slice.73
  11.1 0.9 fusion.7
  12.1 0.1 stack.36
  12.1 0.8 slice.72
  13.0 0.6 pad.15.refs_6_.refs_10_
  13.6 0.2 copy.41
  13.8 0.8 pad.13.refs_3_.refs_2_
  14.6 43.5 %spread_weights.1 = (bf16[4,8,32,1152]{3,2,1,0:T(8,128)(2,1)}, bf16[8,128,1024]{2,1,0:T(8,128)(2,1)}) custom-call(f32[32,4384]{1,0:T(8,128)} %refs_0_.1, f32[32,2048]{1,0:T(8,128)} %refs_1_.1, f32[128,1024]{1,0:T(8,128)} %bitcast.50, f32[1,1024]{1,0:T(1,128)} %bitcast.66), custom_call_target="tpu_custom_call" | custom-call | tf_op jit(solution)/shard_map/spread_weights/pallas_call | solution.py:422
  58.2 30.3 %forward.1 = (f32[1024,256]{1,0:T(8,128)}, f32[1032,512]{1,0:T(8,128)}, f32[1024,128]{1,0:T(8,128)}, bf16[1024,512]{1,0:T(8,128)(2,1)}, f32[1024,256]{1,0:T(8,12...) custom-call(bf16[1024,1024]{1,0:T(8,128)(2,1)} %bitcast.46, bf16[1024,1152]{1,0:T(8,128)(2,1)} %bitcast.43, ...), custom_call_target="tpu_custom_call" | custom-call | flops 2415919104 | bytes 8388608 | tf_op jit(solution)/shard_map/forward/pallas_call | solution.py:526
  88.5 18.8 %middle.1 = (bf16[4,128,1024]{2,1,0:T(8,128)(2,1)}, f32[1024,256]{1,0:T(8,128)}, bf16[1024,256]{1,0:T(8,128)(2,1)}, bf16[1024,512]{1,0:T(8,128)(2,1)}, f32[128,1...) custom-call(bf16[1024,1024]{1,0:T(8,128)(2,1)} %bitcast.49, bf16[1024,1152]{1,0:T(8,128)(2,1)} %bitcast.44, ...), custom_call_target="tpu_custom_call" | custom-call | flops 2147483648 | bytes 8388608 | tf_op jit(solution)/shard_map/middle/pallas_call | solution.py:526
  107.3 27.0 %backward.1 = (bf16[1024,640]{1,0:T(8,128)(2,1)}, f32[8,128]{1,0:T(8,128)}, f32[8,512]{1,0:T(8,128)}, bf16[8,32,512]{2,1,0:T(8,128)(2,1)}, f32[128,1024]{1,0:T(8,128)}) custom-call(bf16[1024,512]{1,0:T(8,128)(2,1)} %get-tuple-element.41.refs_3_.refs_0_, f32[1024,128]{1,0:T(8,128)} %get-tuple-element.42.refs_1_, f32[1032,8]{1,0:T(8,128)} %pad.13.refs_3_.refs_2_, ...), custom_call_target="tpu_custom_call" | custom-call | flops 536870912 | bytes 8388608 | tf_op jit(solution)/shard_map/backward/pallas_call | solution.py:526
  134.3 0.0 copy-start.10
  134.3 0.0 copy-start.11
  134.3 0.0 copy-start.12
  134.4 48.6 %final.1 = (bf16[8,32,640]{2,1,0:T(8,128)(2,1)}, bf16[8,32,512]{2,1,0:T(8,128)(2,1)}, f32[256,128]{1,0:T(8,128)}, f32[128,1024]{1,0:T(8,128)}) custom-call(bf16[1024,256]{1,0:T(8,128)(2,1)} %get-tuple-element.53.refs_0_, bf16[1024,640]{1,0:T(8,128)(2,1)} %get-tuple-element.54.refs_1_, bf16[1024,1152]{1,0:T(8,128)(2,1)} %bitcast.45, ...), custom_call_target="tpu_custom_call" | custom-call | flops 2684354560 | bytes 8388608 | tf_op jit(solution)/shard_map/final/pallas_call | solution.py:526
  183.0 0.0 copy-start.7
  183.0 0.0 copy-done.10
  183.0 0.0 copy-done.11
  183.0 0.0 copy-done.12
  183.0 1.6 divide_subtract_fusion.2
  184.6 1.0 convert_element_type.64
  185.6 0.0 copy-start.2
  185.7 0.0 copy-start.8
  185.7 0.0 copy-start.9
  185.7 0.0 copy-start.1
  185.7 0.0 copy-done.7
  185.8 0.0 copy-start
  185.8 0.0 copy-start.3
  185.8 0.0 copy-start.4
  185.9 0.1 copy.44
  186.0 0.1 copy.45
  186.1 0.5 copy-done.2
  186.6 0.2 copy-done.8
  186.8 0.1 copy-done.9
  186.9 1.0 divide_subtract_fusion.1
  187.8 0.0 copy-done.1
  187.8 0.0 copy-done
  187.8 0.0 copy-done.3
  187.8 0.0 copy-done.4
  187.8 0.0 copy-start.5
  187.9 0.0 copy-start.6
  187.9 1.5 divide_subtract_fusion
  189.4 0.0 copy-done.5
  189.4 0.8 copy.52
  190.2 0.0 copy-done.6
  190.2 0.8 copy.53
  (13 shorter events, 0.3 us)
Async XLA Ops:
  134.3 48.7 %copy-start.10 = (f32[14688]{0:T(1024)S(1)}, f32[14688]{0:T(1024)}, u32[]{:S(2)}) copy-start(f32[14688]{0:T(1024)} %param.21) | copy-start | bytes 176260
  134.3 48.7 %copy-start.11 = (f32[14688]{0:T(1024)S(1)}, f32[14688]{0:T(1024)}, u32[]{:S(2)}) copy-start(f32[14688]{0:T(1024)} %param.22) | copy-start | bytes 176260
  134.3 48.7 %copy-start.12 = (f32[14688]{0:T(1024)S(1)}, f32[14688]{0:T(1024)}, u32[]{:S(2)}) copy-start(f32[14688]{0:T(1024)} %param.23) | copy-start | bytes 176260
  183.0 2.8 %copy-start.7 = (bf16[8,32,640]{2,1,0:T(8,128)(2,1)S(1)}, bf16[8,32,640]{2,1,0:T(8,128)(2,1)}, u32[]{:S(2)}) copy-start(bf16[8,32,640]{2,1,0:T(8,128)(2,1)} %get-tuple-element.62) | copy-start | bytes 983044
  185.6 1.0 copy-start.2
  185.7 1.1 copy-start.8
  185.7 1.2 copy-start.9
  185.7 2.1 %copy-start.1 = (f32[8,4,8,256]{3,2,0,1:T(8,128)}, f32[8,4,8,256]{3,2,0,1:T(8,128)S(1)}, u32[]{:S(2)}) copy-start(f32[8,4,8,256]{3,2,0,1:T(8,128)S(1)} %copy.49) | copy-start | bytes 786436
  185.8 2.1 %copy-start = (f32[32,4384]{1,0:T(8,128)S(1)}, f32[32,4384]{1,0:T(8,128)}, u32[]{:S(2)}) copy-start(f32[32,4384]{1,0:T(8,128)} %refs_0_.1) | copy-start | bytes 1683460
  185.8 2.1 %copy-start.3 = (f32[32,4384]{1,0:T(8,128)S(1)}, f32[32,4384]{1,0:T(8,128)}, u32[]{:S(2)}) copy-start(f32[32,4384]{1,0:T(8,128)} %param.17) | copy-start | bytes 1683460
  185.8 2.1 %copy-start.4 = (f32[32,4384]{1,0:T(8,128)S(1)}, f32[32,4384]{1,0:T(8,128)}, u32[]{:S(2)}) copy-start(f32[32,4384]{1,0:T(8,128)} %param.18) | copy-start | bytes 1683460
  187.8 1.5 copy-start.5
  187.9 2.3 %copy-start.6 = (f32[128,1024]{1,0:T(8,128)S(1)}, f32[128,1024]{1,0:T(8,128)}, u32[]{:S(2)}) copy-start(f32[128,1024]{1,0:T(8,128)} %get-tuple-element.60) | copy-start | bytes 1572868
where the time goes:
time: 192 us; the launch traced here: 191 us
  Pallas kernels  168 us (88%)
  local copies, waits for them, and re-layouts  12.3 us (6%)
  other arithmetic  9.41 us (5%)
    pallas_call x4, Pallas kernels, call(): pl.pallas_call(kernel, out_shape=outs, in_specs=[in_vmem] * len(operands)...  125 us
    pallas_call x1, Pallas kernels, spread_weights(): pl.pallas_call(lambda *refs: spread_kernel(seq_count, dp_count, *refs), o...  43.5 us
    sub x3, other arithmetic, adamw_update(): param * (1.0 - learn_rate * decay_rate) - learn_rate * corrected / scaled  4.04 us

commit v1 on v0

--- a/solution.py
+++ b/solution.py
@@ -23,20 +23,6 @@
 decay_rate = 0.1
 adam_eps = 1e-08
 top_precision = lax.Precision.HIGHEST
-
-
-def unpack(vector):
-    cursor = D + DI
-    norm_gain = vector[:D]
-    gate_gain = vector[D:cursor]
-    conv_kernel = vector[cursor : cursor + KW * CONV].reshape(KW, CONV)
-    cursor = cursor + KW * CONV
-    conv_bias = vector[cursor : cursor + CONV]
-    cursor = cursor + CONV
-    step_bias = vector[cursor : cursor + H]
-    log_rate = vector[cursor + H : cursor + 2 * H]
-    skip_gain = vector[cursor + 2 * H : cursor + 3 * H]
-    return (norm_gain, gate_gain, conv_kernel, conv_bias, step_bias, log_rate, skip_gain)
 
 
 def input_norm(inputs, gain):
@@ -106,19 +92,6 @@
             rows_index, cols_index, reach, tail, scores, decay_of)
 
 
-def position_table(ids, ext_ids):
-    length = ids.shape[0]
-    chunked = ids.reshape(-1, CHUNK)
-    none = jnp.full((1,), -1, jnp.int32)
-    prior = jnp.concatenate([none, chunked[:-1, -1]])[:, None]
-    following = jnp.concatenate([chunked[1:, 0], none])[:, None]
-    last = chunked[:, -1:]
-    columns = [chunked, chunked == prior, chunked == last, chunked == following]
-    columns = [column.astype(f32).reshape(-1) for column in columns]
-    valid = [(ext_ids[offset : offset + length] == ids).astype(f32) for offset in range(KW - 1)]
-    return jnp.pad(jnp.stack(columns + valid + [jnp.ones_like(columns[0])], axis=1), ((0, 8), (0, 0)))
-
-
 MESH = pl.DeviceIdType.MESH
 in_vmem = pl.BlockSpec(memory_space=pltpu.VMEM)
 
@@ -288,7 +261,57 @@
     return [pltpu.VMEM(block, bf16)] * 4 + [sems((chips,))] * 4
 
 
-def spread_kernel(seq_count, dp_count, in_ref, last_ref, tok_ref, gain_ref, out, normed, blocks,
+def fill_tables(seq_count, vec_ref, ids_ref, table, id_rows, small, kern, gain, skip):
+    here = lax.axis_index("seq")
+    width = DI // seq_count
+    heads = H // seq_count
+    base = D + DI
+    gain[...] = vec_ref[:, pl.ds(pl.multiple_of(D + here * width, LANES), width)]
+    kern[...] = jnp.zeros_like(kern)
+    for k in range(KW + 1):
+        start = base + k * CONV
+        kern[k : k + 1, :width] = vec_ref[:, pl.ds(pl.multiple_of(start + here * width, LANES), width)]
+        kern[k : k + 1, width:] = vec_ref[:, start + DI : start + CONV]
+    base += (KW + 1) * CONV
+    per_head = jnp.broadcast_to(vec_ref[:, base : base + 3 * H], (8, 3 * H))
+
+    def pick(chosen):
+        return jnp.dot(per_head, chosen.astype(f32), precision=top_precision, preferred_element_type=f32)
+
+    source = lax.broadcasted_iota(jnp.int32, (3 * H, LANES), 0)
+    target = lax.broadcasted_iota(jnp.int32, (3 * H, LANES), 1)
+    line = lax.broadcasted_iota(jnp.int32, (8, LANES), 0)
+    bias, rate = [pick((source == target + k * H + here * heads) & (target < heads)) for k in (0, 1)]
+    small[...] = jnp.where(line == 0, bias, jnp.where(line == 1, rate, 0.0))
+    head = lax.broadcasted_iota(jnp.int32, (3 * H, width), 0) - 2 * H - here * heads
+    spot = lax.broadcasted_iota(jnp.int32, (3 * H, width), 1)
+    skip[...] = pick((spot >= head * P_SIZE) & (spot < (head + 1) * P_SIZE))[0:1, :]
+    ids = ids_ref[...].astype(f32)
+    length = ids.shape[1]
+    tall = jnp.broadcast_to(ids, (8, length))
+    lane = lax.broadcasted_iota(jnp.int32, (8, length), 1)
+    valid = []
+    for k in range(KW - 1):
+        shift = KW - 1 - k
+        valid.append((pltpu.roll(tall, shift, 1) == tall) & (lane >= shift))
+    none = jnp.full((1, 1), -1.0, f32)
+    count = length // CHUNK
+    for c in range(count):
+        low, high = c * CHUNK, (c + 1) * CHUNK
+        block = tall[:, low:high]
+        prior = ids[:, low - 1 : low] if c else none
+        after = ids[:, high : high + 1] if c + 1 < count else none
+        columns = [block == prior, block == ids[:, high - 1 : high], block == after]
+        columns += [v[:, low:high] for v in valid]
+        merged = jnp.where(line == 0, block, 1.0)
+        for k, column in enumerate(columns):
+            merged = jnp.where((line == k + 1) & jnp.logical_not(column), 0.0, merged)
+        table[low:high, :] = merged.T
+        id_rows[c : c + 1, :] = ids[:, low:high]
+    table[length:, :] = jnp.zeros((8, 8), f32)
+
+
+def spread_kernel(seq_count, dp_count, in_ref, last_ref, tok_ref, vec_ref, ids_ref, out, normed, table, id_rows, small, kern, gain, skip, blocks,
                   seq_send, seq_recv, dp_send, dp_recv, right_send, right_recv, left_send, left_recv,
                   core_send, core_recv):
     here, row = lax.axis_index("seq"), lax.axis_index("dp")
@@ -318,11 +341,11 @@
         seq_copy(step, beyond("seq", step), here).start()
         return 0
 
+    begin, stage, finish_rows = row_gather(seq_count, normed, right_send, right_recv, left_send, left_recv, core_send, core_recv)
     lax.fori_loop(1, seq_count, launch, 0)
     out[row, here] = blocks[here]
-    normed[here] = input_norm(tok_ref[...], gain_ref[...][0]).astype(bf16)
-
-    begin, stage, finish_rows = row_gather(seq_count, normed, right_send, right_recv, left_send, left_recv, core_send, core_recv)
+    normed[here] = input_norm(tok_ref[...], vec_ref[0, :D]).astype(bf16)
+
     quads = dp_count == 4
 
     def dp_copy(step, hop, from_row, source_ref):
@@ -375,6 +398,7 @@
     spread_own(0, True)
 
     begin()
+    fill_tables(seq_count, vec_ref, ids_ref, table, id_rows, small, kern, gain, skip)
 
     def forward(step, _):
         seq_copy(step, beyond("seq", step), beyond("seq", -step)).wait_recv()
@@ -383,7 +407,6 @@
         return 0
 
     lax.fori_loop(1, seq_count, forward, 0)
-
     for k in range(1, chips):
         stage(k)
         if k == 1:
@@ -412,26 +435,21 @@
     finish_rows()
 
 
-def spread_weights(in_weight, out_weight, inputs, gain):
+def spread_weights(in_weight, out_weight, inputs, vec, ids):
     seq_count, dp_count = lax.axis_size("seq"), lax.axis_size("dp")
     sems = pltpu.SemaphoreType.DMA
     width = DI // seq_count
     columns = 3 * width + 2 * N + LANES
     block = (seq_count, in_weight.shape[0], columns)
     chips = (seq_count // 2,)
-    return pl.pallas_call(
-        lambda *refs: spread_kernel(seq_count, dp_count, *refs),
-        out_shape=[
-            jax.ShapeDtypeStruct((dp_count,) + block, bf16),
-            jax.ShapeDtypeStruct((seq_count,) + inputs.shape, bf16),
-        ],
-        in_specs=[in_vmem] * 4,
-        out_specs=[in_vmem] * 2,
-        scratch_shapes=[pltpu.VMEM(block, bf16)]
-        + [sems((seq_count,))] * 2 + [sems((seq_count, dp_count))] * 2 + [sems(chips)] * 6,
-        compiler_params=pltpu.CompilerParams(collective_id=1, has_side_effects=True),
-        name="spread_weights",
-    )(in_weight, out_weight, inputs, gain[None, :])
+    length = ids.shape[1]
+    outs = shapes(
+        ((dp_count,) + block, bf16), ((seq_count,) + inputs.shape, bf16), ((length + 8, 8), f32), ((length // CHUNK, CHUNK), f32),
+        ((8, LANES), f32), ((8, width + 2 * N), f32), ((1, width), f32), ((1, width), f32),
+    )
+    scratch = [pltpu.VMEM(block, bf16)] + [sems((seq_count,))] * 2 + [sems((seq_count, dp_count))] * 2 + [sems(chips)] * 6
+    return call(lambda *refs: spread_kernel(seq_count, dp_count, *refs), "spread_weights", 1, outs, scratch,
+                (in_weight, out_weight, inputs, vec, ids), 0)
 
 
 def rows_at(index, size):
@@ -476,7 +494,7 @@
     state[...] = jnp.zeros_like(state)
     arrive()
     begin()
-    tall = 2 * CHUNK
+    tall = 4 * CHUNK
 
     def project(i, _):
         out = contract(normed[rows_at(i, tall), :], weights[:, :in_width], 1, 0)
@@ -509,11 +527,11 @@
         state[...] = entry * wide_reach[CHUNK - 1 :, :] + contract(input_map, weighted, 0, 0)
         return 0
 
-    parts = segments(length // CHUNK, chips)
+    parts = segments(length // CHUNK, max(chips - 1, 1))
     for k, (low, high) in enumerate(parts):
-        lax.fori_loop(low, high, chunk, 0)
         if k + 1 < chips:
             stage(k + 1)
+        lax.fori_loop(low, high, chunk, 0)
     finish()
 
 
@@ -551,9 +569,49 @@
                 (normed, weights, cotangent, table, ids, small, kern), 2 * length * D * weights.shape[1])
 
 
+def trade(term, total, theirs, got, send, recv, partner):
+    block = 2 * CHUNK
+    blocks = D // block
+
+    def move(b):
+        at = rows_at(b, block)
+        return push(theirs.at[:, :, at], got.at[:, :, at], send.at[b], recv.at[b], "seq", partner)
+
+    def give(b, _):
+        theirs[:, :, rows_at(b, block)] = term(0, b).astype(bf16)
+
+        @pl.when(b > 0)
+        def _():
+            move(b - 1).start()
+
+        return 0
+
+    lax.fori_loop(0, blocks, give, 0)
+
+    def keep(b, _):
+        own = term(1, b)
+
+        @pl.when(b == 0)
+        def _():
+            move(blocks - 1).start()
+
+        move(b).wait_recv()
+        at = rows_at(b, block)
+        total[:, :, at] = (own + got[:, :, at].astype(f32)).astype(bf16)
+        return 0
+
+    lax.fori_loop(0, blocks, keep, 0)
+
+    def sent(b, _):
+        move(b).wait_send()
+        return 0
+
+    lax.fori_loop(0, blocks, sent, 0)
+
+
 def middle_kernel(seq_count, upstream, weights, ssd_ref, mixed_ref, gate_ref, gain_ref, skip_ref, normed,
                   total, grad_ref, low_ref, early, scale_ref, gain_grad, norm_row,
-                  product_ref, gg_ref, part, arrived, theirs, got, out_low, send, recv, stat_send, stat_recv):
+                  product_ref, gg_ref, part, arrived, theirs, got, out_low, sorted_ref, send, recv, stat_send, stat_recv):
     width = DI // seq_count
     here = lax.axis_index("seq")
     chips = seq_count // 2
@@ -562,7 +620,8 @@
     length = upstream.shape[0]
     count = length // CHUNK
     first = weights.shape[1] - width
-    tall = 2 * CHUNK
+    tall = 4 * CHUNK
+    block = 2 * CHUNK
     arrive = greet_all(("seq",))
     part[...] = jnp.zeros_like(part)
     line = lax.broadcasted_iota(jnp.int32, (2 * count, width), 0)
@@ -578,10 +637,10 @@
         square = product * product
         crossed = gg * gain_ref[...] * product
         sums = part[...]
-        for half in range(2):
+        for half in range(4):
             rows = slice(half * CHUNK, (half + 1) * CHUNK)
             for offset, value in ((0, square), (count, crossed)):
-                chosen = (line == 2 * i + half + offset).astype(f32)
+                chosen = (line == 4 * i + half + offset).astype(f32)
                 sums = sums + lax.dot_general(chosen, value[rows], (((1,), (1,)), ((), ())), precision=top_precision, preferred_element_type=f32)
         part[...] = sums
         return 0
@@ -597,36 +656,14 @@
     arrived[0] = part[...]
     long = total.shape[1]
 
-    def term(piece):
-        raw_out = (product_ref[rows_at(piece, long), :] * gain_ref[...]).astype(bf16)
-        return contract(raw_out, weights[:, first:], 1, 1)
-
-    def exchange(j):
-        return push(theirs.at[j], got.at[j], send.at[j], recv.at[j], "seq", partner)
-
-    def give(j, _):
-        theirs[j] = term(2 * j + 1 - core).astype(bf16)
-
-        @pl.when(j > 0)
-        def _():
-            exchange(j - 1).start()
-
-        return 0
-
-    lax.fori_loop(0, chips, give, 0)
-
-    def keep(j, _):
-        own = term(2 * j + core)
-
-        @pl.when(j == 0)
-        def _():
-            exchange(chips - 1).start()
-
-        exchange(j).wait_recv()
-        total[j] = (own + got[j].astype(f32)).astype(bf16)
-        return 0
-
-    lax.fori_loop(0, chips, keep, 0)
+    for j in range(chips):
+        for side, piece in ((0, 2 * j + 1 - core), (1, 2 * j + core)):
+            sorted_ref[side, j * long : (j + 1) * long, :] = (product_ref[rows_at(piece, long), :] * gain_ref[...]).astype(bf16)
+
+    def term(side, b):
+        return contract(sorted_ref[side], weights[rows_at(b, block), first:], 1, 1).reshape(chips, long, block)
+
+    trade(term, total, theirs, got, send, recv, partner)
     for copy in copies:
         copy.wait_recv()
     final = arrived[here]
@@ -669,8 +706,6 @@
         return 0
 
     lax.fori_loop(0, D // tall, weigh, 0)
-    for j in range(chips):
-        exchange(j).wait_send()
     for copy in copies:
         copy.wait_send()
 
@@ -695,7 +730,8 @@
     scratch = [
         pltpu.VMEM((length, width), f32), pltpu.VMEM((length, width), f32), pltpu.VMEM((2 * count, CHUNK), f32),
         pltpu.VMEM((seq_count, 2 * count, CHUNK), f32), pltpu.VMEM(block, bf16), pltpu.VMEM(block, bf16),
-        pltpu.VMEM((length, width), bf16), sems((chips,)), sems((chips,)), sems((seq_count,)), sems((seq_count,)),
+        pltpu.VMEM((length, width), bf16), pltpu.VMEM((2, length // 2, width), bf16),
+        sems((D // (2 * CHUNK),)), sems((D // (2 * CHUNK),)), sems((seq_count,)), sems((seq_count,)),
     ]
     return call(lambda *refs: middle_kernel(seq_count, *refs), "middle", 4, outs, scratch,
                 (upstream, weights, ssd, mixed, gate_in, gain, skip, normed), 8 * length * D * width)
@@ -845,7 +881,7 @@
 def final_kernel(seq_count, dp_count, lines, low_ref, late_ref, weights, normed, early, gain_ref, norm_row, gain_grad,
                  gkern_ref, totals_ref, tok_ref, cot_ref,
                  returned, returned_early, vec_out, in_grad_ref,
-                 total, theirs, got_rows, part, got, summed, vec, vec_dp, vec_row, vec_seq, acc,
+                 total, theirs, got_rows, sorted_ref, part, got, summed, vec, vec_dp, vec_row, vec_seq, acc,
                  pair_send, pair_recv, dp_send, dp_recv, seq_send, seq_recv, early_send, early_recv,
                  va_send, va_recv, vb_send, vb_recv, vc_send, vc_recv, vd_send, vd_recv, *chain):
     here, row = lax.axis_index("seq"), lax.axis_index("dp")
@@ -858,7 +894,7 @@
     partner = here + 1 - 2 * core
     hops = range(1, dp_count)
     steps = range(1, seq_count)
-    tall = 2 * CHUNK
+    tall = 4 * CHUNK
     share = part.shape[1]
     begin, slot, finish_rows = row_scatter(seq_count, total, *chain)
     arrive = greet_all(("seq", "dp"))
@@ -874,36 +910,15 @@
 
     long = total.shape[1]
 
-    def term(piece):
-        at = rows_at(piece, long)
-        return contract(low_ref[at, :], weights[:, :width], 1, 1) + contract(late_ref[at, :], weights[:, width:in_width], 1, 1)
-
-    def pair(j):
-        return push(theirs.at[j], got_rows.at[j], pair_send.at[j], pair_recv.at[j], "seq", partner)
-
-    def give(j, _):
-        theirs[j] = term(2 * j + 1 - core).astype(bf16)
-
-        @pl.when(j > 0)
-        def _():
-            pair(j - 1).start()
-
-        return 0
-
-    lax.fori_loop(0, chips, give, 0)
-
-    def keep(j, _):
-        own = term(2 * j + core)
-
-        @pl.when(j == 0)
-        def _():
-            pair(chips - 1).start()
-
-        pair(j).wait_recv()
-        total[j] = (own + got_rows[j].astype(f32)).astype(bf16)
-        return 0
-
-    lax.fori_loop(0, chips, keep, 0)
+    for j in range(chips):
+        for side, piece in ((0, 2 * j + 1 - core), (1, 2 * j + core)):
+            sorted_ref[side, j * long : (j + 1) * long, :width] = low_ref[rows_at(piece, long), :]
+            sorted_ref[side, j * long : (j + 1) * long, width:] = late_ref[rows_at(piece, long), :]
+
+    def term(side, b):
+        return contract(sorted_ref[side], weights[rows_at(b, 2 * CHUNK), :in_width], 1, 1).reshape(chips, long, 2 * CHUNK)
+
+    trade(term, total, theirs, got_rows, pair_send, pair_recv, partner)
     begin()
 
     vec[...] = jnp.zeros_like(vec)
@@ -992,6 +1007,8 @@
 
     half = seq_count // 2
     lax.fori_loop(1, half, swap, 0)
+    for t in range(2, chips - 1):
+        slot(t)
     for copy in second:
         copy.wait_recv()
     final = vec_row[rows_at(here, lines), :]
@@ -1006,8 +1023,6 @@
 
     for step in steps:
         third(step, here).start()
-    for t in range(2, chips - 1):
-        slot(t)
     lax.fori_loop(half, seq_count, swap, 0)
     returned[here] = combined(0)
     for step in steps:
@@ -1021,7 +1036,7 @@
     finish_rows(acc)
     inputs = tok_ref[...]
     scale = lax.rsqrt(jnp.mean(inputs * inputs, axis=-1, keepdims=True) + norm_eps)
-    pulled = acc[...] * gain_ref[...]
+    pulled = acc[...] * gain_ref[:, :D]
     dots = jnp.sum(pulled * inputs, axis=-1, keepdims=True)
     in_grad_ref[...] = cot_ref[...] + scale * pulled - inputs * (scale * scale * scale * dots / D)
 
@@ -1047,8 +1062,6 @@
         copy.wait_send()
     for step in steps:
         third(step, here).wait_send()
-    for j in range(chips):
-        pair(j).wait_send()
 
 
 def final(low, late, weights, normed, early, gain, norm_row, gain_grad, gkern, totals, tokens, cotangent):
@@ -1065,12 +1078,13 @@
         ((seq_count, share, columns), bf16), (early.shape, bf16), ((devices * lines, LANES), f32), (tokens.shape, f32)
     )
     scratch = [
-        pltpu.VMEM(block, bf16), pltpu.VMEM(block, bf16), pltpu.VMEM(block, bf16), pltpu.VMEM((devices, share, columns), bf16),
+        pltpu.VMEM(block, bf16), pltpu.VMEM(block, bf16), pltpu.VMEM(block, bf16),
+        pltpu.VMEM((2, late.shape[0] // 2, low.shape[1] + columns), bf16), pltpu.VMEM((devices, share, columns), bf16),
         pltpu.VMEM((dp_count, seq_count, share, columns), bf16), pltpu.VMEM((seq_count, share, columns), bf16),
         pltpu.VMEM((devices * lines, LANES), f32), pltpu.VMEM((dp_count, seq_count * lines, LANES), f32),
         pltpu.VMEM((seq_count * lines, LANES), f32), pltpu.VMEM((seq_count, lines, LANES), f32), pltpu.VMEM(tokens.shape, f32),
     ]
-    counts = [(chips,)] * 2 + [(seq_count, dp_count)] * 2 + [(seq_count,)] * 4 + [(dp_count,)] * 2 + [(seq_count,)] * 4 + [(dp_count,)] * 2
+    counts = [(D // (2 * CHUNK),)] * 2 + [(seq_count, dp_count)] * 2 + [(seq_count,)] * 4 + [(dp_count,)] * 2 + [(seq_count,)] * 4 + [(dp_count,)] * 2
     scratch += [sems(shape) for shape in counts] + scatter_scratch(block, chips)
     return call(lambda *refs: final_kernel(seq_count, dp_count, lines, *refs), "final", 3, outs, scratch,
                 (low, late, weights, normed, early, gain, norm_row, gain_grad, gkern, totals, tokens, cotangent),
@@ -1079,33 +1093,19 @@
 
 def body(tokens, cotangent, doc_ids, in_weight, out_weight, in_m, in_v, out_m, out_v, vec_params, vec_m, vec_v):
     seq_count = lax.axis_size("seq")
-    place = lax.axis_index("seq")
     heads = H // seq_count
     width = DI // seq_count
     mixed_width = width + 2 * N
     owner_rows = in_weight.shape[0]
     inputs = tokens[0]
     upstream_f = cotangent[0]
-    norm_gain = vec_params[:D]
-
-    weights, normed_all = spread_weights(in_weight, out_weight, inputs, norm_gain)
+
+    vec = vec_params[None, :]
+    weights, normed_all, table, ids_rows, small, kern, own_gain, wide_skip = spread_weights(
+        in_weight, out_weight, inputs, vec, doc_ids
+    )
     weights = weights.reshape(D, -1)
     normed_all = normed_all.reshape(-1, D)
-    _, gate_gain, conv_kernel, conv_bias, step_bias, log_rate, skip_gain = unpack(vec_params)
-    ids = doc_ids[0]
-    ext_ids = jnp.concatenate([jnp.full((KW - 1,), -1, jnp.int32), ids])
-    table = position_table(ids, ext_ids)
-    ids_rows = ids.astype(f32).reshape(-1, CHUNK)
-
-    def own(vector, size):
-        return lax.dynamic_slice_in_dim(vector, place * size, size, vector.ndim - 1)
-
-    own_gain = own(gate_gain, width)[None, :]
-    both = jnp.concatenate([conv_kernel, conv_bias[None, :]])
-    kern = jnp.pad(jnp.concatenate([own(both[:, :DI], width), both[:, DI:]], axis=1), ((0, 7 - KW), (0, 0)))
-    wide_skip = jnp.repeat(own(skip_gain, heads), P_SIZE)[None, :]
-    small = jnp.pad(jnp.stack([own(step_bias, heads), own(log_rate, heads)]), ((0, 6), (0, LANES - heads)))
-
     gate_in, conv_in, raw, mixed, ssd, entries, upstream_all = forward(
         normed_all, weights, upstream_f, table, ids_rows, small, kern
     )
@@ -1118,7 +1118,7 @@
         mixed, raw, table, ids_rows, small, wide_skip, ssd, entries, grad_ssd, conv_in, kern, out_total, early, scale, inputs
     )
     returned, returned_early, vec_sum, input_grad = final(
-        gate_low, late, weights, normed_all, early, norm_gain[None, :], norm_row, gain_grad, gkern, totals, inputs, upstream_f
+        gate_low, late, weights, normed_all, early, vec, norm_row, gain_grad, gkern, totals, inputs, upstream_f
     )
     returned = returned.astype(f32)
     returned_early = returned_early.astype(f32)

time: 192 us -> 177 us (0.922)
  local copies, waits for them, and re-layouts: 12.3 us -> 4.19 us
  other arithmetic: 9.41 us -> 5.12 us
  Pallas kernels: 168 us -> 165 us
    pallas_call x1 -> x0, Pallas kernels: 43.5 us -> none  [spread_weights(): pl.pallas_call(lambda *refs: spread_kernel(seq_count, dp_count, *refs), o...]
    pallas_call x4 -> x5, Pallas kernels: 125 us -> 165 us  [call(): pl.pallas_call(kernel, out_shape=outs, in_specs=[in_vmem] * len(operands)...]
    slice x8 -> x0, local copies, waits for them, and re-layouts: 6.2 us -> none  [the longest x1 1.28 us: body(): norm_gain = vec_params[:D]]
    convert_element_type x3 -> x0, other arithmetic: 2.67 us -> none  [the longest x2 1.39 us: position_table(): columns = [column.astype(f32).reshape(-1) for column in columns]]
where the time goes in v1:
time: 177 us; the launch traced here: 176 us
  Pallas kernels  165 us (93%)
  other arithmetic  5.12 us (3%)
  local copies, waits for them, and re-layouts  4.19 us (2%)
    pallas_call x5, Pallas kernels, call(): pl.pallas_call(kernel, out_shape=outs, in_specs=[in_vmem] * len(operands)...  165 us
    sub x3, other arithmetic, adamw_update(): param * (1.0 - learn_rate * decay_rate) - learn_rate * corrected / scaled  4.04 us

profile of v1, /device:TPU:1, one launch (start us, length us, event | category | flops | bytes accessed | tf_op | source)
XLA Modules:
  0.0 175.7 jit_solution(10111991883747845740)
XLA Ops:
  0.6 1.5 broadcast_in_dim.9.refs_3_.refs_5_
  2.1 43.7 %spread_weights.1 = (bf16[4,8,32,1152]{3,2,1,0:T(8,128)(2,1)}, bf16[8,128,1024]{2,1,0:T(8,128)(2,1)}, f32[1032,8]{1,0:T(8,128)}, f32[8,128]{1,0:T(8,128)}, f32[8...) custom-call(f32[32,4384]{1,0:T(8,128)} %refs_0_.1, f32[32,2048]{1,0:T(8,128)} %refs_1_.1, ...), custom_call_target="tpu_custom_call" | custom-call | bytes 8388608 | tf_op jit(solution)/shard_map/spread_weights/pallas_call | solution.py:544
  45.8 30.2 %forward.1 = (f32[1024,256]{1,0:T(8,128)}, f32[1032,512]{1,0:T(8,128)}, f32[1024,128]{1,0:T(8,128)}, bf16[1024,512]{1,0:T(8,128)(2,1)}, f32[1024,256]{1,0:T(8,12...) custom-call(bf16[1024,1024]{1,0:T(8,128)(2,1)} %bitcast.27, bf16[1024,1152]{1,0:T(8,128)(2,1)} %bitcast.24, ...), custom_call_target="tpu_custom_call" | custom-call | flops 2415919104 | bytes 8388608 | tf_op jit(solution)/shard_map/forward/pallas_call | solution.py:544
  76.1 18.1 %middle.1 = (bf16[4,128,1024]{2,1,0:T(8,128)(2,1)}, f32[1024,256]{1,0:T(8,128)}, bf16[1024,256]{1,0:T(8,128)(2,1)}, bf16[1024,512]{1,0:T(8,128)(2,1)}, f32[128,1...) custom-call(bf16[1024,1024]{1,0:T(8,128)(2,1)} %bitcast.30, bf16[1024,1152]{1,0:T(8,128)(2,1)} %bitcast.25, ...), custom_call_target="tpu_custom_call" | custom-call | flops 2147483648 | bytes 8388608 | tf_op jit(solution)/shard_map/middle/pallas_call | solution.py:544
  94.2 27.3 %backward.1 = (bf16[1024,640]{1,0:T(8,128)(2,1)}, f32[8,128]{1,0:T(8,128)}, f32[8,512]{1,0:T(8,128)}, bf16[8,32,512]{2,1,0:T(8,128)(2,1)}, f32[128,1024]{1,0:T(8,128)}) custom-call(bf16[1024,512]{1,0:T(8,128)(2,1)} %get-tuple-element.51.refs_3_.refs_0_, f32[1024,128]{1,0:T(8,128)} %get-tuple-element.52.refs_1_, f32[1032,8]{1,0:T(8,128)} %get-tuple-element.47.refs_3_.refs_2_, ...), custom_call_target="tpu_custom_call" | custom-call | flops 536870912 | bytes 8388608 | tf_op jit(solution)/shard_map/backward/pallas_call | solution.py:544
  121.5 0.0 copy-start.10
  121.5 0.0 copy-start.11
  121.5 0.0 copy-start.12
  121.5 46.2 %final.1 = (bf16[8,32,640]{2,1,0:T(8,128)(2,1)}, bf16[8,32,512]{2,1,0:T(8,128)(2,1)}, f32[256,128]{1,0:T(8,128)}, f32[128,1024]{1,0:T(8,128)}) custom-call(bf16[1024,256]{1,0:T(8,128)(2,1)} %get-tuple-element.65.refs_0_, bf16[1024,640]{1,0:T(8,128)(2,1)} %get-tuple-element.66.refs_1_, bf16[1024,1152]{1,0:T(8,128)(2,1)} %bitcast.26, ...), custom_call_target="tpu_custom_call" | custom-call | flops 2684354560 | bytes 8388608 | tf_op jit(solution)/shard_map/final/pallas_call | solution.py:544
  167.7 0.0 copy-start.7
  167.7 0.0 copy-done.10
  167.7 0.0 copy-done.11
  167.7 0.0 copy-done.12
  167.7 1.6 divide_subtract_fusion.2
  169.3 1.0 convert_element_type.6
  170.4 0.0 copy-start.2
  170.4 0.0 copy-start.8
  170.4 0.0 copy-start.9
  170.4 0.0 copy-start.1
  170.5 0.0 copy-done.7
  170.5 0.0 copy-start
  170.5 0.0 copy-start.3
  170.5 0.0 copy-start.4
  170.6 0.1 copy.28
  170.7 0.1 copy.29
  170.9 0.5 copy-done.2
  171.3 0.2 copy-done.8
  171.5 0.1 copy-done.9
  171.6 1.0 divide_subtract_fusion.1
  172.6 0.0 copy-done.1
  172.6 0.0 copy-done
  172.6 0.0 copy-done.3
  172.6 0.0 copy-done.4
  172.6 0.0 copy-start.5
  172.6 0.0 copy-start.6
  172.6 1.5 divide_subtract_fusion
  174.1 0.0 copy-done.5
  174.1 0.8 copy.36
  174.9 0.0 copy-done.6
  174.9 0.8 copy.37
  (7 shorter events, 0.2 us)
Async XLA Ops:
  121.5 46.2 %copy-start.10 = (f32[14688]{0:T(1024)S(1)}, f32[14688]{0:T(1024)}, u32[]{:S(2)}) copy-start(f32[14688]{0:T(1024)} %param.21) | copy-start | bytes 176260
  121.5 46.2 %copy-start.11 = (f32[14688]{0:T(1024)S(1)}, f32[14688]{0:T(1024)}, u32[]{:S(2)}) copy-start(f32[14688]{0:T(1024)} %param.22) | copy-start | bytes 176260
  121.5 46.2 %copy-start.12 = (f32[14688]{0:T(1024)S(1)}, f32[14688]{0:T(1024)}, u32[]{:S(2)}) copy-start(f32[14688]{0:T(1024)} %param.23) | copy-start | bytes 176260
  167.7 2.8 %copy-start.7 = (bf16[8,32,640]{2,1,0:T(8,128)(2,1)S(1)}, bf16[8,32,640]{2,1,0:T(8,128)(2,1)}, u32[]{:S(2)}) copy-start(bf16[8,32,640]{2,1,0:T(8,128)(2,1)} %get-tuple-element.74) | copy-start | bytes 983044
  170.4 1.0 copy-start.2
  170.4 1.1 copy-start.8
  170.4 1.2 copy-start.9
  170.4 2.1 %copy-start.1 = (f32[8,4,8,256]{3,2,0,1:T(8,128)}, f32[8,4,8,256]{3,2,0,1:T(8,128)S(1)}, u32[]{:S(2)}) copy-start(f32[8,4,8,256]{3,2,0,1:T(8,128)S(1)} %copy.33) | copy-start | bytes 786436
  170.5 2.1 %copy-start = (f32[32,4384]{1,0:T(8,128)S(1)}, f32[32,4384]{1,0:T(8,128)}, u32[]{:S(2)}) copy-start(f32[32,4384]{1,0:T(8,128)} %refs_0_.1) | copy-start | bytes 1683460
  170.5 2.1 %copy-start.3 = (f32[32,4384]{1,0:T(8,128)S(1)}, f32[32,4384]{1,0:T(8,128)}, u32[]{:S(2)}) copy-start(f32[32,4384]{1,0:T(8,128)} %param.17) | copy-start | bytes 1683460
  170.5 2.1 %copy-start.4 = (f32[32,4384]{1,0:T(8,128)S(1)}, f32[32,4384]{1,0:T(8,128)}, u32[]{:S(2)}) copy-start(f32[32,4384]{1,0:T(8,128)} %param.18) | copy-start | bytes 1683460
  172.6 1.5 copy-start.5
  172.6 2.3 %copy-start.6 = (f32[128,1024]{1,0:T(8,128)S(1)}, f32[128,1024]{1,0:T(8,128)}, u32[]{:S(2)}) copy-start(f32[128,1024]{1,0:T(8,128)} %get-tuple-element.72) | copy-start | bytes 1572868
